TPU v7x, 32 devices: a whole 2x2x4 slice. The times are simulated.
32 devices in a mesh: row: 8 (over y, x, core), col: 4 (over z).
Axes of the slice: x: 2, y: 2, z: 4, core: 2. Of those that a mesh axis runs over, the one named last changes fastest.
Arguments:
- tile_values: bfloat16 [8, 4, 64, 128, 128], P('row', 'col'), may hold values from -0.0625 to 0.0625
- tile_row: int32 [8, 4, 64], P('row', 'col'), may hold values from 0 to 3
- tile_col: int32 [8, 4, 64], P('row', 'col'), may hold values from 0 to 3
- tile_count: int32 [8, 4], P('row', 'col'), may hold values from 16 to 64, as said below
- primal_init: float32 [64, 2048], P(None, ('row', 'col')), may hold values from -3 to 3
- dual_init: float32 [64, 4096], P(None, ('row', 'col')), may hold values from -3 to 3
- cost_vector: float32 [2048], P(('row', 'col')), may hold values from -4 to 4
- lower_bound: float32 [2048], P(('row', 'col')), may hold values from -1 to -0.2
- upper_bound: float32 [2048], P(('row', 'col')), may hold values from 0.2 to 1
- bound_kind: int32 [2048], P(('row', 'col')), may hold values from 0 to 2
- row_kind: int32 [4096], P(('row', 'col')), may hold values from 0 to 1
- demand: float32 [64, 4096], P(None, ('row', 'col')), may hold values from -20 to 20
Outputs:
- primal_out: float32 [64, 2048], P(None, ('row', 'col'))
- dual_out: float32 [64, 4096], P(None, ('row', 'col'))
- residual_norm: float32 [3, 64], replicated
Inputs may be any that keep to these rules, and one draw needn't show every extreme that they name: `tile_count`: live tile slots of one device; some device has all 64 slots live.
All inputs are finite; a program needn't handle non-finite values.
Results may differ from a plain program's by a relative error of at most 0.0022.
Values may be sent and summed in bfloat16 or wider, within the bound.
A program may use at most 64 MiB of HBM per device.

v0:
```python
import jax
import jax.numpy as jnp
from jax import lax
from jax.sharding import PartitionSpec as P

ITERS = 3
PRIMAL_STEP = 0.4
DUAL_STEP = 0.4
NORM_EPS = 1e-06


def block_sum(onehot, product):
    return jnp.einsum("tr,sti->sri", onehot, product, precision=lax.Precision.HIGHEST)


def shards(
    tile_values,
    tile_row,
    tile_col,
    tile_count,
    primal_init,
    dual_init,
    cost_vector,
    lower_bound,
    upper_bound,
    bound_kind,
    row_kind,
    demand,
):
    blocks = tile_values[0, 0]
    slot_rows = tile_row[0, 0]
    slot_cols = tile_col[0, 0]
    live_count = tile_count[0, 0]
    slots = blocks.shape[0]
    tile_size = blocks.shape[-1]
    scenarios = primal_init.shape[0]
    row_devices = lax.axis_size("row")
    col_devices = lax.axis_size("col")
    col_blocks = row_devices // 2
    live_mask = jnp.arange(slots, dtype=jnp.int32) < live_count
    row_onehot = (
        (slot_rows[:, None] == jnp.arange(col_devices, dtype=jnp.int32)[None, :])
        & live_mask[:, None]
    ).astype(jnp.float32)
    col_onehot = (
        (slot_cols[:, None] == jnp.arange(col_blocks, dtype=jnp.int32)[None, :])
        & live_mask[:, None]
    ).astype(jnp.float32)
    total_rows = row_devices * col_devices * tile_size
    inequality = (row_kind == 1).astype(jnp.float32)
    primal = primal_init
    dual = dual_init
    partial_norms = []
    for iteration in range(ITERS):
        dual_half = lax.all_gather(dual.astype(jnp.bfloat16), "col", axis=1, tiled=True)
        grouped = dual_half.reshape(scenarios, col_devices, tile_size)
        picked = jnp.take(grouped, slot_rows, axis=1)
        product = jnp.einsum("tij,sti->stj", blocks, picked, preferred_element_type=jnp.float32)
        summed = block_sum(col_onehot, product)
        summed = summed.reshape(scenarios, col_blocks * tile_size)
        transposed = lax.psum_scatter(summed, "row", scatter_dimension=1, tiled=True)
        primal_next = primal - PRIMAL_STEP * (cost_vector[None, :] - transposed)
        primal_next = jnp.where(
            (bound_kind <= 1)[None, :], jnp.maximum(primal_next, lower_bound[None, :]), primal_next
        )
        primal_next = jnp.where(
            (bound_kind == 0)[None, :], jnp.minimum(primal_next, upper_bound[None, :]), primal_next
        )
        extrapolated = (2.0 * primal_next - primal).astype(jnp.bfloat16)
        gathered = lax.all_gather(extrapolated, "row", axis=1, tiled=True)
        apply_grouped = gathered.reshape(scenarios, col_blocks, tile_size)
        apply_picked = jnp.take(apply_grouped, slot_cols, axis=1)
        apply_product = jnp.einsum(
            "tij,stj->sti", blocks, apply_picked, preferred_element_type=jnp.float32
        )
        apply_summed = block_sum(row_onehot, apply_product)
        partial_value = apply_summed.reshape(scenarios, col_devices * tile_size)
        image = lax.psum_scatter(partial_value, "col", scatter_dimension=1, tiled=True)
        gap_rows = demand - image
        dual = dual + DUAL_STEP * gap_rows
        dual = jnp.where(inequality[None, :] > 0.0, jnp.maximum(dual, 0.0), dual)
        primal = primal_next
        squares = jnp.sum(gap_rows * gap_rows, axis=1)
        partial_norms.append(lax.psum(squares, ("row", "col")))
    totals = jnp.stack(partial_norms)
    residual_norm = jnp.sqrt(totals / total_rows + NORM_EPS)
    return (primal, dual, residual_norm)


def solution(mesh):
    return jax.shard_map(
        shards,
        mesh=mesh,
        in_specs=(
            P("row", "col", None, None, None),
            P("row", "col", None),
            P("row", "col", None),
            P("row", "col"),
            P(None, ("row", "col")),
            P(None, ("row", "col")),
            P(("row", "col")),
            P(("row", "col")),
            P(("row", "col")),
            P(("row", "col")),
            P(("row", "col")),
            P(None, ("row", "col")),
        ),
        out_specs=(P(None, ("row", "col")), P(None, ("row", "col")), P()),
        check_vma=False,
    )
```

profile of v0, /device:TPU:10, one launch (start us, length us, event | category | flops | bytes accessed | tf_op | source)
XLA Modules:
  0.0 312.5 jit_solution(8858715847128932885)
XLA Ops:
  7.2 0.8 compare_and_fusion.1
  8.0 0.7 compare_select_fusion.1
  9.4 0.8 convert_element_type.23
  10.1 12.3 %all_gather.18 = bf16[64,512]{1,0:T(8,128)(2,1)S(1)} all-gather(bf16[64,128]{1,0:T(8,128)(2,1)S(1)} %convert_element_type.23), channel_id=1, replica_groups=mesh['row'=8,'col'=4] {'col'}, dimensions={1}, use_global_device_ids=true | all-gather | bytes 81920 | tf_op jit(solution)/shard_map/all_gather | solution.py:55
  22.5 0.7 gather_fusion
  23.3 0.7 fusion.24
  24.1 2.0 fusion.42
  26.0 0.8 copy.57
  27.0 33.3 %reduce-scatter.19.cloned.1.call-done = f32[64,64]{1,0:T(8,128)} async-done(((f32[512,64]{1,0:T(8,128)}), f32[64,64]{1,0:T(8,128)}) %reduce-scatter.19.cloned.1.call-update) | async-done | bytes 16400
  60.3 0.8 copy.52
  61.3 8.3 %all_gather.19 = bf16[64,512]{0,1:T(8,128)(2,1)S(1)} all-gather(bf16[64,64]{0,1:T(8,128)(2,1)S(1)} %copy.29), channel_id=1, replica_groups=mesh['row'=8,'col'=4] {'row'}, dimensions={1}, use_global_device_ids=true | all-gather | bytes 73728 | tf_op jit(solution)/shard_map/all_gather | solution.py:70
  69.7 0.8 gather_fusion.1
  70.5 1.5 fusion.27
  72.1 2.0 fusion.20
  74.0 0.7 copy.92
  74.8 17.4 %reduce-scatter.13.cloned.1.call-done = f32[64,128]{1,0:T(8,128)} async-done(((f32[64,512]{1,0:T(8,128)}), f32[64,128]{1,0:T(8,128)}) %reduce-scatter.13.cloned.1.call-update) | async-done | bytes 32784 | tf_op jit(solution)/shard_map/reduce_scatter | solution.py:78
  92.2 0.8 fusion.75
  93.0 12.4 %all_gather.20 = bf16[64,512]{1,0:T(8,128)(2,1)S(1)} all-gather(bf16[64,128]{1,0:T(8,128)(2,1)S(1)} %fusion.75), channel_id=1, replica_groups=mesh['row'=8,'col'=4] {'col'}, dimensions={1}, use_global_device_ids=true | all-gather | bytes 81920 | tf_op jit(solution)/shard_map/all_gather | solution.py:55
  105.4 0.7 gather_fusion.2
  106.1 0.7 fusion.30
  106.9 2.0 fusion.45
  108.8 0.8 copy.58
  109.8 34.5 %reduce-scatter.21.cloned.1.call-done = f32[64,64]{1,0:T(8,128)} async-done(((f32[512,64]{1,0:T(8,128)}), f32[64,64]{1,0:T(8,128)}) %reduce-scatter.21.cloned.1.call-update) | async-done | bytes 16400
  144.2 0.8 copy.54
  145.2 8.5 %all_gather.21 = bf16[64,512]{0,1:T(8,128)(2,1)S(1)} all-gather(bf16[64,64]{0,1:T(8,128)(2,1)S(1)} %copy.35), channel_id=1, replica_groups=mesh['row'=8,'col'=4] {'row'}, dimensions={1}, use_global_device_ids=true | all-gather | bytes 73728 | tf_op jit(solution)/shard_map/all_gather | solution.py:70
  153.8 0.8 gather_fusion.3
  154.5 1.5 fusion.33
  156.1 2.0 fusion.16
  158.1 0.7 copy.91
  158.8 17.4 %reduce-scatter.15.cloned.1.call-done = f32[64,128]{1,0:T(8,128)} async-done(((f32[64,512]{1,0:T(8,128)}), f32[64,128]{1,0:T(8,128)}) %reduce-scatter.15.cloned.1.call-update) | async-done | bytes 32784 | tf_op jit(solution)/shard_map/reduce_scatter | solution.py:78
  176.2 0.8 fusion.95
  177.0 12.4 %all_gather.22 = bf16[64,512]{1,0:T(8,128)(2,1)S(1)} all-gather(bf16[64,128]{1,0:T(8,128)(2,1)S(1)} %fusion.95), channel_id=1, replica_groups=mesh['row'=8,'col'=4] {'col'}, dimensions={1}, use_global_device_ids=true | all-gather | bytes 81920 | tf_op jit(solution)/shard_map/all_gather | solution.py:55
  189.4 0.7 gather_fusion.4
  190.2 0.7 fusion.36
  190.9 2.0 fusion.48
  192.8 0.8 copy.59
  193.8 34.5 %reduce-scatter.23.cloned.1.call-done = f32[64,64]{1,0:T(8,128)} async-done(((f32[512,64]{1,0:T(8,128)}), f32[64,64]{1,0:T(8,128)}) %reduce-scatter.23.cloned.1.call-update) | async-done | bytes 16400
  228.2 0.8 copy.56
  229.0 0.7 subtract_convert_fusion
  229.8 8.3 %all_gather.23 = bf16[64,512]{0,1:T(8,128)(2,1)S(1)} all-gather(bf16[64,64]{0,1:T(8,128)(2,1)S(1)} %copy.41), channel_id=1, replica_groups=mesh['row'=8,'col'=4] {'row'}, dimensions={1}, use_global_device_ids=true | all-gather | bytes 73728 | tf_op jit(solution)/shard_map/all_gather | solution.py:70
  238.2 0.8 gather_fusion.5
  239.0 1.5 fusion.39
  240.5 2.0 fusion.12
  242.5 0.7 copy.90
  243.1 17.5 %reduce-scatter.17.cloned.1.call-done = f32[64,128]{1,0:T(8,128)} async-done(((f32[64,512]{1,0:T(8,128)}), f32[64,128]{1,0:T(8,128)}) %reduce-scatter.17.cloned.1.call-update) | async-done | bytes 32784 | tf_op jit(solution)/shard_map/reduce_scatter | solution.py:78
  260.6 1.5 multiply_reduce_fusion.2
  262.1 42.9 %all-reduce = (f32[1,64]{1,0:T(1,128)S(1)}, f32[1,64]{1,0:T(1,128)S(1)}, f32[1,64]{1,0:T(1,128)S(1)}) all-reduce(f32[1,64]{1,0:T(1,128)S(1)} %bitcast.152, f32[1,64]{1,0:T(1,128)S(1)} %bitcast.151, f32[1,64]{1,0:T(1,128)S(1)} %bitcast.150), channel_id=1, replica_groups=mesh['row'=8,'col'=4] {'row','col'}, use_global_device_ids=true, to_apply=%region_11.13 | all-reduce | flops 192 | bytes 1536 | tf_op jit(solution)/shard_map/psum | solution.py:84
  305.1 0.6 fusion.77
  (56 shorter events, 1.1 us)
Async XLA Ops:
  7.2 16.1 %copy-start = (bf16[1,1,64,128,128]{4,3,2,1,0:T(8,128)(2,1)S(1)}, bf16[1,1,64,128,128]{4,3,2,1,0:T(8,128)(2,1)}, u32[]{:S(2)}) copy-start(bf16[1,1,64,128,128]{4,3,2,1,0:T(8,128)(2,1)} %param.14) | copy-start | bytes 6291460
  7.2 53.1 %reduce-scatter.19.cloned.1.call-start = ((), (), s32[]{:S(2)}) async-start(), calls=%async_computation.9 | async-start | bytes 294912
  23.3 0.8 copy-start.9
  24.0 3.0 copy-start.11
  24.0 37.2 %copy-start.4 = (f32[64,64]{1,0:T(8,128)S(1)}, f32[64,64]{1,0:T(8,128)}, u32[]{:S(2)}) copy-start(f32[64,64]{1,0:T(8,128)} %param.18) | copy-start | bytes 49156
  24.0 37.1 %copy-start.6 = (f32[64]{0:T(128)S(1)}, f32[64]{0:T(128)}, u32[]{:S(2)}) copy-start(f32[64]{0:T(128)} %param.22) | copy-start | bytes 772
  24.0 37.1 %copy-start.7 = (f32[64]{0:T(128)S(1)}, f32[64]{0:T(128)}, u32[]{:S(2)}) copy-start(f32[64]{0:T(128)} %param.21) | copy-start | bytes 772
  24.0 37.1 %copy-start.8 = (f32[64]{0:T(128)S(1)}, f32[64]{0:T(128)}, u32[]{:S(2)}) copy-start(f32[64]{0:T(128)} %param.20) | copy-start | bytes 772
  26.9 65.3 %reduce-scatter.13.cloned.1.call-start = ((), (), s32[]{:S(2)}) async-start(), calls=%async_computation.6 | async-start | bytes 163840 | tf_op jit(solution)/shard_map/reduce_scatter | solution.py:78
  70.5 1.6 copy-start.10
  72.0 2.7 copy-start.12
  72.0 20.1 %copy-start.1 = (f32[64,128]{1,0:T(8,128)S(1)}, f32[64,128]{1,0:T(8,128)}, u32[]{:S(2)}) copy-start(f32[64,128]{1,0:T(8,128)} %param.19) | copy-start | bytes 98308
  72.1 20.1 %copy-start.2 = (f32[64,128]{1,0:T(8,128)S(1)}, f32[64,128]{1,0:T(8,128)}, u32[]{:S(2)}) copy-start(f32[64,128]{1,0:T(8,128)} %param.25) | copy-start | bytes 98308
  74.7 69.5 %reduce-scatter.21.cloned.1.call-start = ((), (), s32[]{:S(2)}) async-start(), calls=%async_computation.10 | async-start | bytes 294912
  109.7 66.5 %reduce-scatter.15.cloned.1.call-start = ((), (), s32[]{:S(2)}) async-start(), calls=%async_computation.7 | async-start | bytes 163840 | tf_op jit(solution)/shard_map/reduce_scatter | solution.py:78
  156.1 20.1 %copy-start.3 = (f32[64,128]{1,0:T(8,128)S(1)}, f32[64,128]{1,0:T(8,128)}, u32[]{:S(2)}) copy-start(f32[64,128]{1,0:T(8,128)} %reduce-scatter.13.cloned.1.call-done) | copy-start | bytes 98308
  158.7 69.5 %reduce-scatter.23.cloned.1.call-start = ((), (), s32[]{:S(2)}) async-start(), calls=%async_computation.11 | async-start | bytes 294912
  193.7 66.9 %reduce-scatter.17.cloned.1.call-start = ((), (), s32[]{:S(2)}) async-start(), calls=%async_computation.8 | async-start | bytes 163840 | tf_op jit(solution)/shard_map/reduce_scatter | solution.py:78
  240.5 20.1 %copy-start.5 = (f32[64,128]{1,0:T(8,128)S(1)}, f32[64,128]{1,0:T(8,128)}, u32[]{:S(2)}) copy-start(f32[64,128]{1,0:T(8,128)} %reduce-scatter.15.cloned.1.call-done) | copy-start | bytes 98308
Sparse Core Ops, SparseCore 0:
  27.0 33.2 reduce-scatter.18
  74.8 17.2 reduce-scatter.12
  109.8 34.3 reduce-scatter.20
  158.9 17.2 reduce-scatter.14
  193.8 34.3 reduce-scatter.22
  243.3 17.2 reduce-scatter.16
where the time goes:
time: 313 us
  waiting for transfers between devices  155 us (50%)
  blocking collectives  105 us (34%)
  matrix products  18.5 us (6%)
  between operations  15.1 us (5%)
  local copies, waits for them, and re-layouts  12.2 us (4%)
  other arithmetic  6.66 us (2%)
    unnamed x9, waiting for transfers between devices  102 us
    reduce_scatter x3, waiting for transfers between devices, shards(): lax.psum_scatter(partial_value, 'col', scatter_dimension=1, tiled=True)  52.2 us
    psum x1, blocking collectives, shards(): partial_norms.append(lax.psum(squares, ('row', 'col')))  42.9 us
    all_gather x3, blocking collectives, shards(): lax.all_gather(dual.astype(jnp.bfloat16), 'col', axis=1, tiled=True)  37.2 us
    all_gather x3, blocking collectives, shards(): gathered = lax.all_gather(extrapolated, 'row', axis=1, tiled=True)  25.1 us
    dot_general x6, matrix products, block_sum(): jnp.einsum('tr,sti->sri', onehot, product, precision=lax.Precision.HIGHEST)  11.8 us
    unnamed x35, local copies, waits for them, and re-layouts  7.05 us
  transfers between devices with their start and end apart: 6, of which 6 were waited for; matrix products, arithmetic and copies ran while one was open for 0% of the time, Pallas kernels for 0%

commit v1 on v0

--- a/solution.py
+++ b/solution.py
@@ -7,6 +7,11 @@
 PRIMAL_STEP = 0.4
 DUAL_STEP = 0.4
 NORM_EPS = 1e-06
+
+
+def summed_here(x, axis):
+    blocks = lax.all_gather(x, axis)
+    return jnp.sum(blocks, axis=0)
 
 
 def block_sum(onehot, product):
@@ -81,7 +86,7 @@
         dual = jnp.where(inequality[None, :] > 0.0, jnp.maximum(dual, 0.0), dual)
         primal = primal_next
         squares = jnp.sum(gap_rows * gap_rows, axis=1)
-        partial_norms.append(lax.psum(squares, ("row", "col")))
+        partial_norms.append(summed_here(squares, ("row", "col")))
     totals = jnp.stack(partial_norms)
     residual_norm = jnp.sqrt(totals / total_rows + NORM_EPS)
     return (primal, dual, residual_norm)

time: 313 us -> 314 us (level)
    psum x1 -> x0, blocking collectives: 42.9 us -> none  [shards(): partial_norms.append(lax.psum(squares, ('row', 'col')))]
    unnamed x0 -> x1, blocking collectives: none -> 42.9 us
    unnamed x35 -> x41, local copies, waits for them, and re-layouts: 7.05 us -> 7.81 us
where the time goes in v1:
time: 314 us
  waiting for transfers between devices  155 us (49%)
  blocking collectives  105 us (33%)
  matrix products  18.6 us (6%)
  between operations  15.1 us (5%)
  local copies, waits for them, and re-layouts  13.1 us (4%)
  other arithmetic  6.74 us (2%)
    unnamed x9, waiting for transfers between devices  102 us
    reduce_scatter x3, waiting for transfers between devices, shards(): lax.psum_scatter(partial_value, 'col', scatter_dimension=1, tiled=True)  52.2 us
    unnamed x1, blocking collectives  42.9 us
    all_gather x3, blocking collectives, shards(): lax.all_gather(dual.astype(jnp.bfloat16), 'col', axis=1, tiled=True)  37.2 us
    all_gather x3, blocking collectives, shards(): gathered = lax.all_gather(extrapolated, 'row', axis=1, tiled=True)  25.1 us
    dot_general x6, matrix products, block_sum(): jnp.einsum('tr,sti->sri', onehot, product, precision=lax.Precision.HIGHEST)  11.8 us
    unnamed x41, local copies, waits for them, and re-layouts  7.81 us
  transfers between devices with their start and end apart: 6, of which 6 were waited for; matrix products, arithmetic and copies ran while one was open for 0% of the time, Pallas kernels for 0%

profile of v1, /device:TPU:10, one launch (start us, length us, event | category | flops | bytes accessed | tf_op | source)
XLA Modules:
  0.0 313.6 jit_solution(4479882083796330905)
XLA Ops:
  7.2 0.8 compare_select_fusion.1
  8.0 0.7 compare_and_fusion.1
  9.4 0.8 convert_element_type.23
  10.1 12.3 %all_gather.36 = bf16[64,512]{1,0:T(8,128)(2,1)S(1)} all-gather(bf16[64,128]{1,0:T(8,128)(2,1)S(1)} %convert_element_type.23), channel_id=1, replica_groups=mesh['row'=8,'col'=4] {'col'}, dimensions={1}, use_global_device_ids=true | all-gather | bytes 81920 | tf_op jit(solution)/shard_map/all_gather | solution.py:60
  22.5 0.7 gather_fusion
  23.3 0.7 fusion.24
  24.1 2.0 fusion.42
  26.0 0.8 copy.75
  27.0 33.3 %reduce-scatter.19.cloned.1.call-done = f32[64,64]{1,0:T(8,128)} async-done(((f32[512,64]{1,0:T(8,128)}), f32[64,64]{1,0:T(8,128)}) %reduce-scatter.19.cloned.1.call-update) | async-done | bytes 16400
  60.3 0.8 copy.70
  61.3 8.3 %all_gather.37 = bf16[64,512]{0,1:T(8,128)(2,1)S(1)} all-gather(bf16[64,64]{0,1:T(8,128)(2,1)S(1)} %copy.47), channel_id=1, replica_groups=mesh['row'=8,'col'=4] {'row'}, dimensions={1}, use_global_device_ids=true | all-gather | bytes 73728 | tf_op jit(solution)/shard_map/all_gather | solution.py:75
  69.7 0.8 gather_fusion.1
  70.5 1.5 fusion.27
  72.1 2.0 fusion.20
  74.0 0.6 copy.110
  74.8 17.4 %reduce-scatter.13.cloned.1.call-done = f32[64,128]{1,0:T(8,128)} async-done(((f32[64,512]{1,0:T(8,128)}), f32[64,128]{1,0:T(8,128)}) %reduce-scatter.13.cloned.1.call-update) | async-done | bytes 32784 | tf_op jit(solution)/shard_map/reduce_scatter | solution.py:83
  92.2 0.8 fusion.75
  92.9 12.4 %all_gather.38 = bf16[64,512]{1,0:T(8,128)(2,1)S(1)} all-gather(bf16[64,128]{1,0:T(8,128)(2,1)S(1)} %fusion.75), channel_id=1, replica_groups=mesh['row'=8,'col'=4] {'col'}, dimensions={1}, use_global_device_ids=true | all-gather | bytes 81920 | tf_op jit(solution)/shard_map/all_gather | solution.py:60
  105.4 0.7 gather_fusion.2
  106.1 0.7 fusion.30
  106.9 2.0 fusion.45
  108.8 0.8 copy.76
  109.7 34.5 %reduce-scatter.21.cloned.1.call-done = f32[64,64]{1,0:T(8,128)} async-done(((f32[512,64]{1,0:T(8,128)}), f32[64,64]{1,0:T(8,128)}) %reduce-scatter.21.cloned.1.call-update) | async-done | bytes 16400
  144.2 0.8 copy.72
  145.2 8.5 %all_gather.39 = bf16[64,512]{0,1:T(8,128)(2,1)S(1)} all-gather(bf16[64,64]{0,1:T(8,128)(2,1)S(1)} %copy.53), channel_id=1, replica_groups=mesh['row'=8,'col'=4] {'row'}, dimensions={1}, use_global_device_ids=true | all-gather | bytes 73728 | tf_op jit(solution)/shard_map/all_gather | solution.py:75
  153.8 0.8 gather_fusion.3
  154.5 1.5 fusion.33
  156.1 2.0 fusion.16
  158.0 0.6 copy.109
  158.8 17.4 %reduce-scatter.15.cloned.1.call-done = f32[64,128]{1,0:T(8,128)} async-done(((f32[64,512]{1,0:T(8,128)}), f32[64,128]{1,0:T(8,128)}) %reduce-scatter.15.cloned.1.call-update) | async-done | bytes 32784 | tf_op jit(solution)/shard_map/reduce_scatter | solution.py:83
  176.2 0.8 fusion.95
  176.9 12.4 %all_gather.40 = bf16[64,512]{1,0:T(8,128)(2,1)S(1)} all-gather(bf16[64,128]{1,0:T(8,128)(2,1)S(1)} %fusion.95), channel_id=1, replica_groups=mesh['row'=8,'col'=4] {'col'}, dimensions={1}, use_global_device_ids=true | all-gather | bytes 81920 | tf_op jit(solution)/shard_map/all_gather | solution.py:60
  189.4 0.7 gather_fusion.4
  190.1 0.7 fusion.36
  190.9 2.0 fusion.48
  192.8 0.8 copy.77
  193.7 34.6 %reduce-scatter.23.cloned.1.call-done = f32[64,64]{1,0:T(8,128)} async-done(((f32[512,64]{1,0:T(8,128)}), f32[64,64]{1,0:T(8,128)}) %reduce-scatter.23.cloned.1.call-update) | async-done | bytes 16400
  228.3 0.8 copy.74
  229.1 0.7 subtract_convert_fusion
  229.9 8.3 %all_gather.41 = bf16[64,512]{0,1:T(8,128)(2,1)S(1)} all-gather(bf16[64,64]{0,1:T(8,128)(2,1)S(1)} %copy.59), channel_id=1, replica_groups=mesh['row'=8,'col'=4] {'row'}, dimensions={1}, use_global_device_ids=true | all-gather | bytes 73728 | tf_op jit(solution)/shard_map/all_gather | solution.py:75
  238.3 0.8 gather_fusion.5
  239.0 1.5 fusion.39
  240.6 2.0 fusion.12
  242.5 0.6 copy.108
  243.2 17.4 %reduce-scatter.17.cloned.1.call-done = f32[64,128]{1,0:T(8,128)} async-done(((f32[64,512]{1,0:T(8,128)}), f32[64,128]{1,0:T(8,128)}) %reduce-scatter.17.cloned.1.call-update) | async-done | bytes 32784 | tf_op jit(solution)/shard_map/reduce_scatter | solution.py:83
  260.7 1.5 multiply_reduce_fusion.2
  263.0 42.9 %all-reduce.3 = (f32[2048]{0:T(1024)S(1)}, f32[2048]{0:T(1024)S(1)}, f32[2048]{0:T(1024)S(1)}) all-reduce(f32[2048]{0:T(1024)S(1)} %dynamic-update-slice.2, f32[2048]{0:T(1024)S(1)} %dynamic-update-slice.1, f32[2048]{0:T(1024)S(1)} %dynamic-update-slice), channel_id=4, replica_groups=mesh['row'=8,'col'=4] {'row','col'}, use_global_device_ids=true, to_apply=%add.2 | all-reduce | flops 6144 | bytes 49152
  306.2 0.6 fusion.77
  (68 shorter events, 2.2 us)
Async XLA Ops:
  7.2 16.1 %copy-start = (bf16[1,1,64,128,128]{4,3,2,1,0:T(8,128)(2,1)S(1)}, bf16[1,1,64,128,128]{4,3,2,1,0:T(8,128)(2,1)}, u32[]{:S(2)}) copy-start(bf16[1,1,64,128,128]{4,3,2,1,0:T(8,128)(2,1)} %param.14) | copy-start | bytes 6291460
  7.2 53.1 %reduce-scatter.19.cloned.1.call-start = ((), (), s32[]{:S(2)}) async-start(), calls=%async_computation.9 | async-start | bytes 294912
  23.3 0.8 copy-start.9
  24.0 3.0 copy-start.11
  24.0 37.1 %copy-start.4 = (f32[64,64]{1,0:T(8,128)S(1)}, f32[64,64]{1,0:T(8,128)}, u32[]{:S(2)}) copy-start(f32[64,64]{1,0:T(8,128)} %param.18) | copy-start | bytes 49156
  24.0 37.1 %copy-start.6 = (f32[64]{0:T(128)S(1)}, f32[64]{0:T(128)}, u32[]{:S(2)}) copy-start(f32[64]{0:T(128)} %param.22) | copy-start | bytes 772
  24.0 37.1 %copy-start.7 = (f32[64]{0:T(128)S(1)}, f32[64]{0:T(128)}, u32[]{:S(2)}) copy-start(f32[64]{0:T(128)} %param.21) | copy-start | bytes 772
  24.0 37.1 %copy-start.8 = (f32[64]{0:T(128)S(1)}, f32[64]{0:T(128)}, u32[]{:S(2)}) copy-start(f32[64]{0:T(128)} %param.20) | copy-start | bytes 772
  26.9 65.3 %reduce-scatter.13.cloned.1.call-start = ((), (), s32[]{:S(2)}) async-start(), calls=%async_computation.6 | async-start | bytes 163840 | tf_op jit(solution)/shard_map/reduce_scatter | solution.py:83
  70.5 1.6 copy-start.10
  72.0 2.7 copy-start.12
  72.0 20.1 %copy-start.1 = (f32[64,128]{1,0:T(8,128)S(1)}, f32[64,128]{1,0:T(8,128)}, u32[]{:S(2)}) copy-start(f32[64,128]{1,0:T(8,128)} %param.19) | copy-start | bytes 98308
  72.1 20.1 %copy-start.2 = (f32[64,128]{1,0:T(8,128)S(1)}, f32[64,128]{1,0:T(8,128)}, u32[]{:S(2)}) copy-start(f32[64,128]{1,0:T(8,128)} %param.25) | copy-start | bytes 98308
  74.7 69.5 %reduce-scatter.21.cloned.1.call-start = ((), (), s32[]{:S(2)}) async-start(), calls=%async_computation.10 | async-start | bytes 294912
  109.7 66.5 %reduce-scatter.15.cloned.1.call-start = ((), (), s32[]{:S(2)}) async-start(), calls=%async_computation.7 | async-start | bytes 163840 | tf_op jit(solution)/shard_map/reduce_scatter | solution.py:83
  156.1 20.1 %copy-start.3 = (f32[64,128]{1,0:T(8,128)S(1)}, f32[64,128]{1,0:T(8,128)}, u32[]{:S(2)}) copy-start(f32[64,128]{1,0:T(8,128)} %reduce-scatter.13.cloned.1.call-done) | copy-start | bytes 98308
  158.7 69.6 %reduce-scatter.23.cloned.1.call-start = ((), (), s32[]{:S(2)}) async-start(), calls=%async_computation.11 | async-start | bytes 294912
  193.7 67.0 %reduce-scatter.17.cloned.1.call-start = ((), (), s32[]{:S(2)}) async-start(), calls=%async_computation.8 | async-start | bytes 163840 | tf_op jit(solution)/shard_map/reduce_scatter | solution.py:83
  240.6 20.1 %copy-start.5 = (f32[64,128]{1,0:T(8,128)S(1)}, f32[64,128]{1,0:T(8,128)}, u32[]{:S(2)}) copy-start(f32[64,128]{1,0:T(8,128)} %reduce-scatter.15.cloned.1.call-done) | copy-start | bytes 98308
Sparse Core Ops, SparseCore 0:
  27.0 33.2 reduce-scatter.18
  74.8 17.2 reduce-scatter.12
  109.8 34.3 reduce-scatter.20
  158.8 17.2 reduce-scatter.14
  193.8 34.4 reduce-scatter.22
  243.3 17.2 reduce-scatter.16
